TPU v7x, 1024 devices: a whole 8x8x8 slice. The times are simulated.
1024 devices in a mesh: segment: 64 (over y, z), row: 4 (over x_hi), col: 4 (over x_lo, core).
Axes of the slice: x: 8 (x_hi: 4, x_lo: 2; x = x_hi * 2 + x_lo), y: 8, z: 8, core: 2. Of those that a mesh axis runs over, the one named last changes fastest.
Arguments:
- weights: bfloat16 [64, 4096, 4096], P('segment', 'row', 'col'), may hold values from -0.09375 to 0.09375
- layer_gains: float32 [64, 4096], P('segment', 'col'), may hold values from -0.5 to 0.5
- incoming: bfloat16 [64, 256, 4096], P('segment', 'row', 'col'), may hold values from -6 to 6
- fresh_batch: bfloat16 [256, 4096], P('row', 'col'), may hold values from -6 to 6
- returning: bfloat16 [64, 256, 4096], P('segment', 'row', 'col'), may hold values from -6 to 6
- fresh_cotangent: bfloat16 [256, 4096], P('row', 'col'), may hold values from -6 to 6
- stashed_inputs: bfloat16 [64, 2, 256, 4096], P('segment', None, 'row', 'col'), may hold values from -6 to 6
Outputs:
- layer_outputs: bfloat16 [64, 2, 256, 4096], P('segment', None, 'row', 'col')
- input_grads: bfloat16 [64, 2, 256, 4096], P('segment', None, 'row', 'col')
All inputs are finite; a program needn't handle non-finite values.
Results may differ from a plain program's by a relative error of at most 0.0055.
Values may be sent and summed in bfloat16 or wider, within the bound.
A program may use at most 32 MiB of HBM per device.

v0:
```python
import jax
import jax.numpy as jnp
from jax import lax
from jax.sharding import PartitionSpec as P


def passed_along(value, axis, steps):
    count = lax.axis_size(axis)
    first, last = (max(0, -steps), min(count, count - steps))
    return lax.ppermute(value, axis, [(source, source + steps) for source in range(first, last)])


def silu_slope(values):
    sigma = jax.nn.sigmoid(values)
    return sigma * (1.0 + values * (1.0 - sigma))


def pass_on(message, direction):
    return passed_along(message, "segment", direction)


def widen(pair):
    return (
        lax.all_gather(pair[0], "col", axis=1, tiled=True),
        lax.all_gather(pair[1], "col", axis=1, tiled=True),
    )


def shards(weights, layer_gains, incoming, fresh_batch, returning, fresh_cotangent, stashed_inputs):
    segment_index = lax.axis_index("segment")
    segment_count = lax.axis_size("segment")
    weight_block = weights[0]
    weight_panel = lax.all_gather(weight_block, "row", axis=0, tiled=True)
    layer_gain = layer_gains[0][None, :]

    def advance(own_block, full_input):
        pre_act = jnp.dot(full_input, weight_panel, preferred_element_type=jnp.float32)
        return (own_block.astype(jnp.float32) + layer_gain * jax.nn.silu(pre_act)).astype(
            jnp.bfloat16
        )

    def retreat(upstream, full_stored):
        pre_act = jnp.dot(full_stored, weight_panel, preferred_element_type=jnp.float32)
        scaled = (upstream.astype(jnp.float32) * layer_gain * silu_slope(pre_act)).astype(
            jnp.bfloat16
        )
        partial_terms = lax.dot_general(
            scaled, weight_panel, (((1,), (1,)), ((), ())), preferred_element_type=jnp.float32
        )
        back_term = lax.psum_scatter(
            partial_terms.astype(jnp.bfloat16), "col", scatter_dimension=1, tiled=True
        ).astype(jnp.float32)
        return (upstream.astype(jnp.float32) + back_term).astype(jnp.bfloat16)

    full_input, full_stored = widen((incoming[0], stashed_inputs[0, 0]))
    first_out = advance(incoming[0], full_input)
    grad_first = retreat(returning[0], full_stored)
    arrived = pass_on(first_out, 1)
    feed_block = jnp.where(segment_index == 0, fresh_batch, arrived)
    full_feed, full_second = widen((feed_block, stashed_inputs[0, 1]))
    second_out = advance(feed_block, full_feed)
    arrived_grad = pass_on(grad_first, -1)
    upstream = jnp.where(segment_index == segment_count - 1, fresh_cotangent, arrived_grad)
    grad_second = retreat(upstream, full_second)
    layer_outputs = jnp.stack([first_out, second_out], axis=0)[None]
    input_grads = jnp.stack([grad_first, grad_second], axis=0)[None]
    return (layer_outputs, input_grads)


def solution(mesh):
    in_specs = (
        P("segment", "row", "col"),
        P("segment", "col"),
        P("segment", "row", "col"),
        P("row", "col"),
        P("segment", "row", "col"),
        P("row", "col"),
        P("segment", None, "row", "col"),
    )
    out_specs = (P("segment", None, "row", "col"), P("segment", None, "row", "col"))
    return jax.shard_map(shards, mesh=mesh, in_specs=in_specs, out_specs=out_specs, check_vma=False)
```

profile of v0, /device:TPU:1, one launch (start us, length us, event | category | flops | bytes accessed | tf_op | source)
XLA Modules:
  0.0 280.9 jit_solution(9956974401769230407)
XLA Ops:
  7.2 0.0 all-gather.6.cloned.1.call-start
  7.2 0.7 all-gather.6.cloned.1.call-update
  7.9 0.0 reduce-scatter.3.cloned.1.call-start
  7.9 1.0 fusion.57
  8.9 20.5 %all-gather.2 = bf16[1,1,64,4096]{3,2,1,0:T(8,128)(2,1)S(1)} all-gather(bf16[1,1,64,1024]{3,2,1,0:T(8,128)(2,1)S(1)} %get-tuple-element.2), channel_id=4, replica_groups=mesh['segment'=64,'row'=4,'col'=4] {'col'}, dimensions={3}, use_global_device_ids=true | all-gather | bytes 655360 | tf_op jit(solution)/shard_map/all_gather | solution.py:25
  29.4 154.0 %all-gather.6.cloned.1.call-done = bf16[1,4096,1024]{2,1,0:T(8,128)(2,1)} async-done(((bf16[1,1024,1024]{2,1,0:T(8,128)(2,1)}), bf16[1,4096,1024]{2,1,0:T(8,128)(2,1)}) %all-gather.6.cloned.1.call-update) | async-done | bytes 8388624 | tf_op jit(solution)/shard_map/all_gather | solution.py:33
  183.4 0.0 copy-start.1
  183.4 0.0 copy-start
  183.4 0.0 copy-start.4
  183.4 10.9 %fusion.12 = bf16[64,4096]{1,0:T(8,128)(2,1)} fusion(bf16[1,4096,1024]{2,1,0:T(8,128)(2,1)} %all-gather.6.cloned.1.call-done, bf16[1,1,64,4096]{3,2,1,0:T(8,128)(2,1)S(1)} %all-gather.2, bf16[1,64,1024]{2,1,0:T(8,128)(2,1)} %param.11, f32[1024]{0:T(1024)} %bitcast.72), kind=kOutput, calls=%fused_computation.12 | convolution fusion | flops 1074724864 | bytes 9572352 | tf_op jit(solution)/shard_map/dot_general | solution.py:47
  194.3 0.0 reduce-scatter.3.cloned.1.call-update
  194.3 0.0 reduce-scatter.5.cloned.1.call-start
  194.4 7.3 %all-gather.3 = bf16[1,1,64,4096]{3,2,1,0:T(8,128)(2,1)S(1)} all-gather(bf16[1,1,64,1024]{3,2,1,0:T(8,128)(2,1)S(1)} %get-tuple-element.3), channel_id=5, replica_groups=mesh['segment'=64,'row'=4,'col'=4] {'col'}, dimensions={3}, use_global_device_ids=true | all-gather | bytes 655360 | tf_op jit(solution)/shard_map/all_gather | solution.py:25
  201.6 0.0 copy-done.1
  201.6 7.3 %all-gather = bf16[1,64,4096]{2,1,0:T(8,128)(2,1)S(1)} all-gather(bf16[1,64,1024]{2,1,0:T(8,128)(2,1)S(1)} %copy-done.1), channel_id=2, replica_groups=mesh['segment'=64,'row'=4,'col'=4] {'col'}, dimensions={2}, use_global_device_ids=true | all-gather | bytes 655360 | tf_op jit(solution)/shard_map/all_gather | solution.py:24
  208.9 13.1 %reduce-scatter.3.cloned.1.call-done = bf16[64,1024]{1,0:T(8,128)(2,1)} async-done(((bf16[64,4096]{1,0:T(8,128)(2,1)}), bf16[64,1024]{1,0:T(8,128)(2,1)}) %reduce-scatter.3.cloned.1.call-update) | async-done | bytes 131088 | tf_op jit(solution)/shard_map/reduce_scatter | solution.py:50
  222.0 0.0 copy-done
  222.0 0.9 fusion.26
  223.0 0.0 copy-start.2
  223.0 1.4 collective-permute-start.1
  224.4 0.0 copy-done.4
  224.4 5.0 %fusion.27 = bf16[64,1024]{1,0:T(8,128)(2,1)S(1)} fusion(bf16[1,4096,1024]{2,1,0:T(8,128)(2,1)} %all-gather.6.cloned.1.call-done, bf16[1,64,4096]{2,1,0:T(8,128)(2,1)S(1)} %all-gather, bf16[1,64,1024]{2,1,0:T(8,128)(2,1)S(1)} %copy-done.1, f32[1024]{0:T(1024)S(1)} %bitcast.73), kind=kOutput, calls=%fused_computation.30 | convolution fusion | flops 537395200 | bytes 9179136 | tf_op jit(solution)/shard_map/dot_general | solution.py:37
  229.4 0.0 copy-start.3
  229.5 4.1 %collective-permute-start = (bf16[64,1024]{1,0:T(8,128)(2,1)S(1)}, bf16[64,1024]{1,0:T(8,128)(2,1)S(1)}, u32[]{:S(2)}, u32[]{:S(2)}) collective-permute-start(bf16[64,1024]{1,0:T(8,128)(2,1)S(1)} %fusion.27), channel_id=1, source_target_pairs={{0,16},{16,32},{32,48},{48,64},{64,80},{80,96},{96,112},{112,128},... | collective-permute-start | bytes 393224 | tf_op jit(solution)/shard_map/ppermute | solution.py:10
  233.6 0.0 collective-permute-done.1
  233.6 0.0 copy-done.2
  233.6 10.8 %fusion.15 = bf16[64,4096]{1,0:T(8,128)(2,1)} fusion(bf16[1,4096,1024]{2,1,0:T(8,128)(2,1)} %all-gather.6.cloned.1.call-done, bf16[1,1,64,4096]{3,2,1,0:T(8,128)(2,1)S(1)} %all-gather.3, f32[1024]{0:T(1024)S(1)} %bitcast.74, bf16[64,1024]{1,0:T(8,128)(2,1)S(1)} %copy-done.2, bf16[64,1024]{1,0:T(8,128)(2,1)S(1)} %collective-permute-done.1, pred[]{:T(512)S(6)} %eq.7), kind=kOutput, calls=%fused_computation.13 | convolution fusion | flops 1074790400 | bytes 9703425 | tf_op jit(solution)/shard_map/dot_general | solution.py:47
  244.4 0.0 reduce-scatter.5.cloned.1.call-update
  244.4 0.0 collective-permute-done
  244.4 0.0 copy-done.3
  244.4 7.3 %all_gather.17 = bf16[64,4096]{1,0:T(8,128)(2,1)S(1)} all-gather(bf16[64,1024]{1,0:T(8,128)(2,1)S(1)} %broadcast_select_fusion.1), channel_id=1, replica_groups=mesh['segment'=64,'row'=4,'col'=4] {'col'}, dimensions={1}, use_global_device_ids=true | all-gather | bytes 655360 | tf_op jit(solution)/shard_map/all_gather | solution.py:24
  251.7 5.0 %fusion.54 = bf16[1,64,1024]{2,1,0:T(8,128)(2,1)S(1)} fusion(f32[1024]{0:T(1024)S(1)} %bitcast.75, bf16[64,1024]{1,0:T(8,128)(2,1)S(1)} %broadcast_select_fusion.1, bf16[64,4096]{1,0:T(8,128)(2,1)S(1)} %all_gather.17, bf16[1,4096,1024]{2,1,0:T(8,128)(2,1)} %all-gather.6.cloned.1.call-done), kind=kOutput, calls=%fused_computation.40 | convolution fusion | flops 537395200 | bytes 9179136 | tf_op jit(solution)/shard_map/dot_general | solution.py:37
  256.7 0.7 maximum_bitcast_fusion
  257.5 15.2 %reduce-scatter.5.cloned.1.call-done = bf16[64,1024]{1,0:T(8,128)(2,1)} async-done(((bf16[64,4096]{1,0:T(8,128)(2,1)}), bf16[64,1024]{1,0:T(8,128)(2,1)}) %reduce-scatter.5.cloned.1.call-update) | async-done | bytes 131088 | tf_op jit(solution)/shard_map/reduce_scatter | solution.py:50
  272.6 1.0 fusion.48
  273.6 0.7 maximum_bitcast_fusion.1
  (1 shorter events, 0.0 us)
Async XLA Ops:
  7.2 176.2 %all-gather.6.cloned.1.call-start = ((), (), s32[]{:S(2)}) async-start(), calls=%async_computation.4 | async-start | bytes 10485760 | tf_op jit(solution)/shard_map/all_gather | solution.py:33
  7.9 214.1 %reduce-scatter.3.cloned.1.call-start = ((), (), s32[]{:S(2)}) async-start(), calls=%async_computation.2 | async-start | bytes 655360 | tf_op jit(solution)/shard_map/reduce_scatter | solution.py:50
  183.4 18.3 %copy-start.1 = (bf16[1,64,1024]{2,1,0:T(8,128)(2,1)S(1)}, bf16[1,64,1024]{2,1,0:T(8,128)(2,1)}, u32[]{:S(2)}) copy-start(bf16[1,64,1024]{2,1,0:T(8,128)(2,1)} %param.9) | copy-start | bytes 393220
  183.4 38.7 %copy-start = (bf16[1,64,1024]{2,1,0:T(8,128)(2,1)S(1)}, bf16[1,64,1024]{2,1,0:T(8,128)(2,1)}, u32[]{:S(2)}) copy-start(bf16[1,64,1024]{2,1,0:T(8,128)(2,1)} %param.11) | copy-start | bytes 393220
  183.4 41.0 %copy-start.4 = (f32[1,1024]{1,0:T(1,128)S(1)}, f32[1,1024]{1,0:T(1,128)}, u32[]{:S(2)}) copy-start(f32[1,1024]{1,0:T(1,128)} %param.8) | copy-start | bytes 12292
  194.3 78.3 %reduce-scatter.5.cloned.1.call-start = ((), (), s32[]{:S(2)}) async-start(), calls=%async_computation.3 | async-start | bytes 655360 | tf_op jit(solution)/shard_map/reduce_scatter | solution.py:50
  223.0 10.6 %copy-start.2 = (bf16[64,1024]{1,0:T(8,128)(2,1)S(1)}, bf16[64,1024]{1,0:T(8,128)(2,1)}, u32[]{:S(2)}) copy-start(bf16[64,1024]{1,0:T(8,128)(2,1)} %param.12) | copy-start | bytes 393220
  223.0 10.6 %collective-permute-start.1 = (bf16[64,1024]{1,0:T(8,128)(2,1)S(1)}, bf16[64,1024]{1,0:T(8,128)(2,1)S(1)}, u32[]{:S(2)}, u32[]{:S(2)}) collective-permute-start(bf16[64,1024]{1,0:T(8,128)(2,1)S(1)} %fusion.26), channel_id=1, source_target_pairs={{16,0},{32,16},{48,32},{64,48},{80,64},{96,80},{112,96},{128,112},... | collective-permute-start | bytes 393224 | tf_op jit(solution)/shard_map/ppermute | solution.py:10
  229.4 15.0 %copy-start.3 = (bf16[64,1024]{1,0:T(8,128)(2,1)S(1)}, bf16[64,1024]{1,0:T(8,128)(2,1)}, u32[]{:S(2)}) copy-start(bf16[64,1024]{1,0:T(8,128)(2,1)} %param.10) | copy-start | bytes 393220
  229.5 14.9 %collective-permute-start = (bf16[64,1024]{1,0:T(8,128)(2,1)S(1)}, bf16[64,1024]{1,0:T(8,128)(2,1)S(1)}, u32[]{:S(2)}, u32[]{:S(2)}) collective-permute-start(bf16[64,1024]{1,0:T(8,128)(2,1)S(1)} %fusion.27), channel_id=1, source_target_pairs={{0,16},{16,32},{32,48},{48,64},{64,80},{80,96},{96,112},{112,128},... | collective-permute-start | bytes 393224 | tf_op jit(solution)/shard_map/ppermute | solution.py:10
Sparse Core Ops, SparseCore 0:
  10.7 172.6 all-gather.5
  194.4 27.5 reduce-scatter.2
  244.5 28.0 reduce-scatter.4
where the time goes:
time: 281 us
  waiting for transfers between devices  183 us (65%)
  blocking collectives  42.3 us (15%)
  matrix products  31.7 us (11%)
  between operations  13.9 us (5%)
  starting transfers between devices  5.67 us (2%)
  other arithmetic  3.37 us (1%)
    all_gather x1, waiting for transfers between devices, shards(): weight_panel = lax.all_gather(weight_block, 'row', axis=0, tiled=True)  154 us
    reduce_scatter x2, waiting for transfers between devices, retreat(): lax.psum_scatter(partial_terms.astype(jnp.bfloat16), 'col', scatter_dimen...  28.3 us
    all_gather x2, blocking collectives, widen(): lax.all_gather(pair[1], 'col', axis=1, tiled=True)  27.7 us
    dot_general x2, matrix products, retreat(): lax.dot_general(scaled, weight_panel, (((1,), (1,)), ((), ())), preferred...  21.6 us
    all_gather x2, blocking collectives, widen(): lax.all_gather(pair[0], 'col', axis=1, tiled=True)  14.5 us
    dot_general x2, matrix products, advance(): jnp.dot(full_input, weight_panel, preferred_element_type=jnp.float32)  10 us
  transfers between devices with their start and end apart: 5, of which 3 were waited for; matrix products, arithmetic and copies ran while one was open for 8% of the time, Pallas kernels for 0%

commit v1 on v0

v1 whole, which is shorter than its diff:
```python
import functools

import jax
import jax.numpy as jnp
from jax import lax
from jax.experimental import pallas as pl
from jax.experimental.pallas import tpu as pltpu
from jax.sharding import PartitionSpec as P

MESH = pl.DeviceIdType.MESH
BF16 = jnp.bfloat16
F32 = jnp.float32

BACK1, FWD1, BACK2, FWD2 = range(4)
GATHER, CORE, CROSS, RELAY, HOP_UP, HOP_DOWN, LATE_UP, LATE_DOWN, SUM_UP, SUM_DOWN = range(10)
OWN_UP, OWN_DOWN, REST_UP, REST_DOWN, NEXT_UP, NEXT_DOWN, PART_FAR, PART_NEAR, PAIR, HOME = range(10)
STREAM_COPIES = 10
SEG_OUT, SEG_GRAD = 60, 61
COPIES = 62


def token_of(row, col):
    first = jnp.where(col == 0, 0, jnp.where(col == 1, 3, col - 1))
    last = jnp.where(col == 2, 0, jnp.where(col == 3, 3, col + 1))
    return jnp.where(row == 0, first, jnp.where(row == 3, last, col))


def collector_of(row, token):
    first = jnp.where(token == 0, 0, jnp.where(token == 3, 1, token + 1))
    last = jnp.where(token == 0, 2, jnp.where(token == 3, 3, token - 1))
    return jnp.where(row == 0, first, jnp.where(row == 3, last, token))


def kernel(
    segments,
    gain_ref,
    weight_hbm,
    incoming_hbm,
    fresh_hbm,
    returning_hbm,
    cotangent_hbm,
    stash_hbm,
    outputs_hbm,
    grads_hbm,
    weight,
    incoming,
    fresh,
    returning,
    cotangent,
    full_in,
    partial,
    hop_in,
    hop_out,
    last_in,
    scaled,
    back_partial,
    core_in,
    pair_out,
    pair_in,
    home_out,
    home_in,
    result,
    message,
    feed,
    upstream,
    grad,
    grad_message,
    send_sem,
    recv_sem,
    local_sem,
):
    seg = lax.axis_index("segment")
    row = lax.axis_index("row")
    col = lax.axis_index("col")
    block = incoming.shape[0]
    half = block // 2
    width = incoming.shape[1]
    tile = min(256, width)

    up, down, over = (row + 1) % 4, (row + 3) % 4, (row + 2) % 4
    core = col + 1 - 2 * (col % 2)
    cross = (col + 2) % 4
    both = (core + 2) % 4
    token, token_core, token_cross, token_both = [token_of(row, c) for c in (col, core, cross, both)]
    spot = collector_of(col, row)
    seg_next = (seg + 1) % segments
    seg_prev = (seg + segments - 1) % segments
    diagonal = row == col

    dev_core, dev_cross = (seg, row, core), (seg, row, cross)
    dev_up, dev_down = (seg, up, col), (seg, down, col)
    dev_spot, dev_home = (seg, col, spot), (seg, token, row)

    def rows(ref, index, start=0, size=None):
        size = block if size is None else size
        return ref.at[pl.ds(pl.multiple_of(index * block + start, half), size)]

    def send(key, src, dst, device):
        copy = pltpu.make_async_remote_copy(
            src_ref=src,
            dst_ref=dst,
            send_sem=send_sem.at[key],
            recv_sem=recv_sem.at[key],
            device_id=device,
            device_id_type=MESH,
        )
        copy.start()

    def arrived(key, ref):
        pltpu.make_async_remote_copy(
            src_ref=ref,
            dst_ref=ref,
            send_sem=send_sem.at[key],
            recv_sem=recv_sem.at[key],
            device_id=dev_core,
            device_id_type=MESH,
        ).wait_recv()

    def left(key, ref):
        pltpu.make_async_remote_copy(
            src_ref=ref,
            dst_ref=ref,
            send_sem=send_sem.at[key],
            recv_sem=recv_sem.at[key],
            device_id=dev_core,
            device_id_type=MESH,
        ).wait_send()

    loads = [
        pltpu.make_async_copy(src, dst, local_sem.at[at])
        for at, (src, dst) in enumerate(
            [
                (weight_hbm, weight),
                (incoming_hbm, incoming),
                (returning_hbm, returning),
                (fresh_hbm, fresh),
                (cotangent_hbm, cotangent),
            ]
        )
    ]
    for load in loads:
        load.start()

    barrier = pltpu.get_barrier_semaphore()
    others = [
        dev_core,
        dev_cross,
        dev_up,
        dev_down,
        (seg_next, row, col),
        (seg_prev, row, col),
        (seg_next, col, spot),
        (seg_prev, token, row),
    ]
    for device in others:
        pl.semaphore_signal(barrier, inc=1, device_id=device, device_id_type=MESH)

    @pl.when(diagonal)
    def _():
        pl.semaphore_wait(barrier, len(others))

    @pl.when(jnp.logical_not(diagonal))
    def _():
        for device in (dev_spot, dev_home):
            pl.semaphore_signal(barrier, inc=1, device_id=device, device_id_type=MESH)
        pl.semaphore_wait(barrier, len(others) + 2)

    def key_of(stream, step):
        return stream * STREAM_COPIES + step

    def back_key(tick, step):
        return (4 + tick) * STREAM_COPIES + step

    def gather(stream, source):
        key = key_of(stream, GATHER)
        target = rows(full_in.at[stream], row)

        @pl.when(diagonal)
        def _():
            pltpu.make_async_copy(source, target, recv_sem.at[key]).start()

        @pl.when(jnp.logical_not(diagonal))
        def _():
            send(key, source, target, dev_spot)

    def share(stream):
        mine = rows(full_in.at[stream], token)
        arrived(key_of(stream, GATHER), mine)
        send(key_of(stream, CROSS), mine, mine, dev_cross)
        send(key_of(stream, CORE), mine, mine, dev_core)

    def relay(stream):
        theirs = rows(full_in.at[stream], token_cross)
        arrived(key_of(stream, CROSS), theirs)
        send(key_of(stream, RELAY), theirs, theirs, dev_core)

    def multiply(stream):
        arrived(key_of(stream, CORE), rows(full_in.at[stream], token_core))
        arrived(key_of(stream, RELAY), rows(full_in.at[stream], token_both))

        @pl.loop(0, width // tile)
        def _(step):
            at = pl.ds(pl.multiple_of(step * tile, tile), tile)
            partial[stream, :, at] = jnp.dot(
                full_in[stream], weight[:, at], preferred_element_type=F32
            ).astype(BF16)

        mine, reach, final = partial.at[stream], hop_in.at[stream], last_in.at[stream]
        send(key_of(stream, HOP_UP), rows(mine, over, 0, half), reach.at[0], dev_up)
        send(key_of(stream, HOP_DOWN), rows(mine, over, half, half), reach.at[1], dev_down)
        send(key_of(stream, LATE_UP), rows(mine, up, half, half), final.at[0, pl.ds(half, half)], dev_up)
        send(key_of(stream, LATE_DOWN), rows(mine, down, 0, half), final.at[1, pl.ds(0, half)], dev_down)

    def pass_sum(stream):
        mine, reach, final = partial.at[stream], hop_in.at[stream], last_in.at[stream]
        arrived(key_of(stream, HOP_UP), reach.at[0])
        hop_out[stream, 0] = (reach[0].astype(F32) + rows(mine, up, 0, half)[...].astype(F32)).astype(BF16)
        send(key_of(stream, SUM_UP), hop_out.at[stream, 0], final.at[0, pl.ds(0, half)], dev_up)
        arrived(key_of(stream, HOP_DOWN), reach.at[1])
        hop_out[stream, 1] = (reach[1].astype(F32) + rows(mine, down, half, half)[...].astype(F32)).astype(BF16)
        send(key_of(stream, SUM_DOWN), hop_out.at[stream, 1], final.at[1, pl.ds(half, half)], dev_down)

    def pre_activation(stream):
        final = last_in.at[stream]
        arrived(key_of(stream, LATE_UP), final.at[0, pl.ds(half, half)])
        arrived(key_of(stream, LATE_DOWN), final.at[1, pl.ds(0, half)])
        arrived(key_of(stream, SUM_UP), final.at[0, pl.ds(0, half)])
        arrived(key_of(stream, SUM_DOWN), final.at[1, pl.ds(half, half)])
        own = rows(partial.at[stream], row)[...].astype(F32)
        return own + final[0].astype(F32) + final[1].astype(F32)

    def advance(stream, own_block):
        pre = pre_activation(stream)
        return (own_block.astype(F32) + gain_ref[...] * (pre * jax.nn.sigmoid(pre))).astype(BF16)

    def scale(tick, stream, coming):
        pre = pre_activation(stream)
        sigma = jax.nn.sigmoid(pre)
        slope = sigma * (1.0 + pre * (1.0 - sigma))
        all_rows = scaled.at[tick]
        rows(all_rows, row)[...] = (coming.astype(F32) * gain_ref[...] * slope).astype(BF16)
        low, high = rows(all_rows, row, 0, half), rows(all_rows, row, half, half)
        send(back_key(tick, OWN_UP), low, low, dev_up)
        send(back_key(tick, OWN_DOWN), high, high, dev_down)
        send(back_key(tick, REST_UP), high, high, dev_up)
        send(back_key(tick, REST_DOWN), low, low, dev_down)

    def pass_scaled(tick):
        low, high = rows(scaled.at[tick], down, 0, half), rows(scaled.at[tick], up, half, half)
        arrived(back_key(tick, OWN_UP), low)
        send(back_key(tick, NEXT_UP), low, low, dev_up)
        arrived(back_key(tick, OWN_DOWN), high)
        send(back_key(tick, NEXT_DOWN), high, high, dev_down)

    def multiply_back(tick):
        all_rows = scaled.at[tick]
        arrived(back_key(tick, REST_UP), rows(all_rows, down, half, half))
        arrived(back_key(tick, REST_DOWN), rows(all_rows, up, 0, half))
        arrived(back_key(tick, NEXT_UP), rows(all_rows, over, 0, half))
        arrived(back_key(tick, NEXT_DOWN), rows(all_rows, over, half, half))

        @pl.loop(0, width // tile)
        def _(step):
            at = pl.ds(pl.multiple_of(step * tile, tile), tile)
            back_partial[tick, :, at] = lax.dot_general(
                scaled[tick], weight[at, :], (((1,), (1,)), ((), ())), preferred_element_type=F32
            ).astype(BF16)

        mine = back_partial.at[tick]
        send(back_key(tick, PART_FAR), rows(mine, token_both), core_in.at[tick, 1], dev_core)
        send(back_key(tick, PART_NEAR), rows(mine, token_core), core_in.at[tick, 0], dev_core)

    def pair_sum(tick):
        arrived(back_key(tick, PART_FAR), core_in.at[tick, 1])
        own = rows(back_partial.at[tick], token_cross)[...].astype(F32)
        pair_out[tick] = (own + core_in[tick, 1].astype(F32)).astype(BF16)
        send(back_key(tick, PAIR), pair_out.at[tick], pair_in.at[tick], dev_cross)

    def home_sum(tick):
        arrived(back_key(tick, PART_NEAR), core_in.at[tick, 0])
        arrived(back_key(tick, PAIR), pair_in.at[tick])
        own = rows(back_partial.at[tick], token)[...].astype(F32)
        home_out[tick] = (own + core_in[tick, 0].astype(F32) + pair_in[tick].astype(F32)).astype(BF16)
        key = back_key(tick, HOME)

        @pl.when(diagonal)
        def _():
            pltpu.make_async_copy(home_out.at[tick], home_in.at[tick], recv_sem.at[key]).start()

        @pl.when(jnp.logical_not(diagonal))
        def _():
            send(key, home_out.at[tick], home_in.at[tick], dev_home)

    def gradient(tick, coming):
        arrived(back_key(tick, HOME), home_in.at[tick])
        return (coming.astype(F32) + home_in[tick].astype(F32)).astype(BF16)

    def store(at, src, dst):
        copy = pltpu.make_async_copy(src, dst, local_sem.at[at])
        copy.start()
        return copy

    gather(BACK1, stash_hbm.at[0])
    gather(FWD1, incoming_hbm)
    gather(BACK2, stash_hbm.at[1])
    share(BACK1)
    share(FWD1)
    relay(BACK1)
    for load in loads:
        load.wait()
    relay(FWD1)
    multiply(BACK1)
    multiply(FWD1)
    share(BACK2)
    pass_sum(BACK1)
    relay(BACK2)
    pass_sum(FWD1)
    scale(0, BACK1, returning[...])
    result[0] = advance(FWD1, incoming[...])
    message[...] = jnp.where(seg == segments - 1, fresh[...], result[0])
    send(SEG_OUT, message, feed, (seg_next, row, col))
    send(key_of(FWD2, GATHER), message, rows(full_in.at[FWD2], row), (seg_next, col, spot))
    multiply(BACK2)
    pass_scaled(0)
    stores = [store(5, result.at[0], outputs_hbm.at[0])]
    share(FWD2)
    pass_sum(BACK2)
    multiply_back(0)
    pair_sum(0)
    relay(FWD2)
    home_sum(0)
    multiply(FWD2)
    grad[0] = gradient(0, returning[...])
    grad_message[...] = jnp.where(seg == 0, cotangent[...], grad[0])
    send(SEG_GRAD, grad_message, upstream, (seg_prev, row, col))
    stores.append(store(6, grad.at[0], grads_hbm.at[0]))
    arrived(SEG_GRAD, upstream)
    scale(1, BACK2, upstream[...])
    pass_sum(FWD2)
    pass_scaled(1)
    arrived(SEG_OUT, feed)
    result[1] = advance(FWD2, feed[...])
    stores.append(store(7, result.at[1], outputs_hbm.at[1]))
    multiply_back(1)
    pair_sum(1)
    home_sum(1)
    grad[1] = gradient(1, upstream[...])
    stores.append(store(8, grad.at[1], grads_hbm.at[1]))

    for stream in range(4):
        whole = rows(full_in.at[stream], row)
        if stream != FWD2:

            @pl.when(jnp.logical_not(diagonal))
            def _():
                left(key_of(stream, GATHER), whole)
        else:
            left(key_of(stream, GATHER), whole)
        for step in (CORE, CROSS, RELAY):
            left(key_of(stream, step), whole)
        for step in (HOP_UP, HOP_DOWN, LATE_UP, LATE_DOWN, SUM_UP, SUM_DOWN):
            left(key_of(stream, step), hop_in.at[stream, 0])
    for tick in range(2):
        for step in (OWN_UP, OWN_DOWN, REST_UP, REST_DOWN, NEXT_UP, NEXT_DOWN):
            left(back_key(tick, step), hop_in.at[0, 0])
        for step in (PART_FAR, PART_NEAR, PAIR):
            left(back_key(tick, step), pair_in.at[tick])

        @pl.when(jnp.logical_not(diagonal))
        def _():
            left(back_key(tick, HOME), home_in.at[tick])

    left(SEG_OUT, feed)
    left(SEG_GRAD, upstream)
    for copy in stores:
        copy.wait()


def relay_call(segments, weights, gains, incoming, fresh, returning, cotangent, stashed):
    block, width = incoming.shape
    half, tokens = block // 2, 4 * block
    piece = (block, width)
    hbm = pl.BlockSpec(memory_space=pl.ANY)
    vmem = lambda *shape: pltpu.VMEM(shape, BF16)
    return pl.pallas_call(
        functools.partial(kernel, segments),
        out_shape=[jax.ShapeDtypeStruct((2,) + piece, BF16)] * 2,
        in_specs=[pl.BlockSpec(memory_space=pltpu.VMEM)] + [hbm] * 6,
        out_specs=[hbm] * 2,
        scratch_shapes=[
            vmem(width, width),
            vmem(*piece),
            vmem(*piece),
            vmem(*piece),
            vmem(*piece),
            vmem(4, tokens, width),
            vmem(4, tokens, width),
            vmem(4, 2, half, width),
            vmem(4, 2, half, width),
            vmem(4, 2, block, width),
            vmem(2, tokens, width),
            vmem(2, tokens, width),
            vmem(2, 2, block, width),
            vmem(2, block, width),
            vmem(2, block, width),
            vmem(2, block, width),
            vmem(2, block, width),
            vmem(2, block, width),
            vmem(*piece),
            vmem(*piece),
            vmem(*piece),
            vmem(2, block, width),
            vmem(*piece),
            pltpu.SemaphoreType.DMA((COPIES,)),
            pltpu.SemaphoreType.DMA((COPIES,)),
            pltpu.SemaphoreType.DMA((9,)),
        ],
        compiler_params=pltpu.CompilerParams(collective_id=0, has_side_effects=True),
    )(gains, weights, incoming, fresh, returning, cotangent, stashed)


def solution(mesh):
    segments = mesh.shape["segment"]

    def shards(weights, layer_gains, incoming, fresh_batch, returning, fresh_cotangent, stashed_inputs):
        outputs, grads = relay_call(
            segments,
            weights[0],
            layer_gains,
            incoming[0],
            fresh_batch,
            returning[0],
            fresh_cotangent,
            stashed_inputs[0],
        )
        return outputs[None], grads[None]

    in_specs = (
        P("segment", "row", "col"),
        P("segment", "col"),
        P("segment", "row", "col"),
        P("row", "col"),
        P("segment", "row", "col"),
        P("row", "col"),
        P("segment", None, "row", "col"),
    )
    out_specs = (P("segment", None, "row", "col"), P("segment", None, "row", "col"))
    return jax.shard_map(shards, mesh=mesh, in_specs=in_specs, out_specs=out_specs, check_vma=False)
```

time: 281 us -> 132 us (0.47)
  waiting for transfers between devices: 183 us -> 0 us
  Pallas kernels: 0 us -> 126 us
  blocking collectives: 42.3 us -> 0 us
  matrix products: 31.7 us -> 0 us
  between operations: 13.9 us -> 0.64 us
  starting transfers between devices: 5.67 us -> 0 us
  other arithmetic: 3.37 us -> 0 us
    all_gather x1 -> x0, waiting for transfers between devices: 154 us -> none  [shards(): weight_panel = lax.all_gather(weight_block, 'row', axis=0, tiled=True)]
    pallas_call x0 -> x1, Pallas kernels: none -> 126 us  [relay_call(): pl.pallas_call(functools.partial(kernel, segments), out_shape=[jax.ShapeD...]
    all_gather x4 -> x0, blocking collectives: 42.3 us -> none  [the longest x2 27.7 us: widen(): lax.all_gather(pair[1], 'col', axis=1, tiled=True)]
    dot_general x4 -> x0, matrix products: 31.7 us -> none  [the longest x2 21.6 us: retreat(): lax.dot_general(scaled, weight_panel, (((1,), (1,)), ((), ())), preferred...]
    reduce_scatter x2 -> x0, waiting for transfers between devices: 28.3 us -> none  [retreat(): lax.psum_scatter(partial_terms.astype(jnp.bfloat16), 'col', scatter_dimen...]
    ppermute x2 -> x0, starting transfers between devices: 5.55 us -> none  [passed_along(): lax.ppermute(value, axis, [(source, source + steps) for source in range(f...]
    unnamed x10 -> x2, local copies, waits for them, and re-layouts: 0.02 us -> 3.34 us
  transfers between devices with their start and end apart: 5 -> 0, of which waited for: 3 -> 0; matrix products, arithmetic and copies ran while one was open for 8% -> 0% of each run, Pallas kernels for 0% -> 0%
where the time goes in v1:
time: 132 us; the launch traced here: 130 us
  Pallas kernels  126 us (95%)
  local copies, waits for them, and re-layouts  3.34 us (3%)
    pallas_call x1, Pallas kernels, relay_call(): pl.pallas_call(functools.partial(kernel, segments), out_shape=[jax.ShapeD...  126 us
    unnamed x2, local copies, waits for them, and re-layouts  3.34 us

profile of v1, /device:TPU:1, one launch (start us, length us, event | category | flops | bytes accessed | tf_op | source)
XLA Modules:
  0.0 130.5 jit_solution(13508987451787001632)
XLA Ops:
  0.6 126.5 %shard_map.86 = (bf16[2,64,1024]{2,1,0:T(8,128)(2,1)}, bf16[2,64,1024]{2,1,0:T(8,128)(2,1)}) custom-call(f32[1,1024]{1,0:T(1,128)} %gain_ref.1, bf16[1024,1024]{1,0:T(8,128)(2,1)} %bitcast.6, bf16[64,1024]{1,0:T(8,128)(2,1)} %bitcast.10, bf16[64,1024]{1,0:T(8,128)(2,1)} %fresh_hbm.1, bf16[64,1024]{1,0:T(8,128)(2,1)} %bitcast.11, ...), custom_call_target="tpu_custom_call" | custom-call | tf_op jit(solution)/shard_map/pallas_call | solution.py:385
  127.1 1.7 %copy.11 = bf16[1,2,64,1024]{3,2,1,0:T(8,128)(2,1)} copy(bf16[1,2,64,1024]{3,2,1,0:T(8,128)(2,1)} %bitcast.8) | data formatting | bytes 524288
  128.8 1.7 %copy.12 = bf16[1,2,64,1024]{3,2,1,0:T(8,128)(2,1)} copy(bf16[1,2,64,1024]{3,2,1,0:T(8,128)(2,1)} %bitcast.7) | data formatting | bytes 524288

commit v2 on v1

--- a/solution.py
+++ b/solution.py
@@ -12,11 +12,14 @@
 F32 = jnp.float32
 
 BACK1, FWD1, BACK2, FWD2 = range(4)
-GATHER, CORE, CROSS, RELAY, HOP_UP, HOP_DOWN, LATE_UP, LATE_DOWN, SUM_UP, SUM_DOWN = range(10)
-OWN_UP, OWN_DOWN, REST_UP, REST_DOWN, NEXT_UP, NEXT_DOWN, PART_FAR, PART_NEAR, PAIR, HOME = range(10)
-STREAM_COPIES = 10
-SEG_OUT, SEG_GRAD = 60, 61
-COPIES = 62
+GATHER, CROSS, RELAY, CORE, HOP_UP, HOP_DOWN, LATE_UP, LATE_DOWN, SUM_UP, SUM_DOWN = 0, 2, 4, 6, 7, 8, 9, 10, 11, 12
+STREAM_COPIES = 13
+OWN_UP, OWN_DOWN, REST_UP, REST_DOWN, NEXT_UP, NEXT_DOWN, PART_NEAR, PART_FAR, PAIR, HOME = 0, 1, 2, 3, 4, 5, 6, 7, 9, 11
+BACK_COPIES = 13
+BACK_START = 4 * STREAM_COPIES
+SEG_OUT = BACK_START + 2 * BACK_COPIES
+SEG_RETURNING, SEG_TERM = SEG_OUT + 1, SEG_OUT + 2
+COPIES = SEG_OUT + 3
 
 
 def token_of(row, col):
@@ -64,10 +67,12 @@
     feed,
     upstream,
     grad,
-    grad_message,
+    returning_next,
+    term,
     send_sem,
     recv_sem,
     local_sem,
+    here_sem,
 ):
     seg = lax.axis_index("segment")
     row = lax.axis_index("row")
@@ -95,7 +100,10 @@
         size = block if size is None else size
         return ref.at[pl.ds(pl.multiple_of(index * block + start, half), size)]
 
+    sent = {}
+
     def send(key, src, dst, device):
+        sent[key] = dst.shape[0] == half
         copy = pltpu.make_async_remote_copy(
             src_ref=src,
             dst_ref=dst,
@@ -142,16 +150,7 @@
         load.start()
 
     barrier = pltpu.get_barrier_semaphore()
-    others = [
-        dev_core,
-        dev_cross,
-        dev_up,
-        dev_down,
-        (seg_next, row, col),
-        (seg_prev, row, col),
-        (seg_next, col, spot),
-        (seg_prev, token, row),
-    ]
+    others = [dev_core, dev_cross, dev_up, dev_down, (seg_prev, row, col), (seg_prev, token, row)]
     for device in others:
         pl.semaphore_signal(barrier, inc=1, device_id=device, device_id_type=MESH)
 
@@ -165,38 +164,49 @@
             pl.semaphore_signal(barrier, inc=1, device_id=device, device_id_type=MESH)
         pl.semaphore_wait(barrier, len(others) + 2)
 
+    for device in ((seg_next, row, col), (seg_next, col, spot)):
+        pl.semaphore_signal(here_sem, inc=1, device_id=device, device_id_type=MESH)
+
     def key_of(stream, step):
         return stream * STREAM_COPIES + step
 
     def back_key(tick, step):
-        return (4 + tick) * STREAM_COPIES + step
+        return BACK_START + tick * BACK_COPIES + step
 
     def gather(stream, source):
-        key = key_of(stream, GATHER)
-        target = rows(full_in.at[stream], row)
+        def pieces():
+            for part in range(2):
+                piece = source.at[pl.ds(part * half, half)]
+                yield key_of(stream, GATHER) + part, piece, rows(full_in.at[stream], row, part * half, half)
 
         @pl.when(diagonal)
         def _():
-            pltpu.make_async_copy(source, target, recv_sem.at[key]).start()
+            for key, piece, target in pieces():
+                pltpu.make_async_copy(piece, target, recv_sem.at[key]).start()
 
         @pl.when(jnp.logical_not(diagonal))
         def _():
-            send(key, source, target, dev_spot)
+            for key, piece, target in pieces():
+                send(key, piece, target, dev_spot)
 
     def share(stream):
+        for part in range(2):
+            mine = rows(full_in.at[stream], token, part * half, half)
+            arrived(key_of(stream, GATHER) + part, mine)
+            send(key_of(stream, CROSS) + part, mine, mine, dev_cross)
         mine = rows(full_in.at[stream], token)
-        arrived(key_of(stream, GATHER), mine)
-        send(key_of(stream, CROSS), mine, mine, dev_cross)
         send(key_of(stream, CORE), mine, mine, dev_core)
 
     def relay(stream):
-        theirs = rows(full_in.at[stream], token_cross)
-        arrived(key_of(stream, CROSS), theirs)
-        send(key_of(stream, RELAY), theirs, theirs, dev_core)
+        for part in range(2):
+            theirs = rows(full_in.at[stream], token_cross, part * half, half)
+            arrived(key_of(stream, CROSS) + part, theirs)
+            send(key_of(stream, RELAY) + part, theirs, theirs, dev_core)
 
     def multiply(stream):
         arrived(key_of(stream, CORE), rows(full_in.at[stream], token_core))
-        arrived(key_of(stream, RELAY), rows(full_in.at[stream], token_both))
+        for part in range(2):
+            arrived(key_of(stream, RELAY) + part, rows(full_in.at[stream], token_both, part * half, half))
 
         @pl.loop(0, width // tile)
         def _(step):
@@ -267,111 +277,139 @@
             ).astype(BF16)
 
         mine = back_partial.at[tick]
-        send(back_key(tick, PART_FAR), rows(mine, token_both), core_in.at[tick, 1], dev_core)
+        for part in range(2):
+            far = core_in.at[tick, 1, pl.ds(part * half, half)]
+            send(back_key(tick, PART_FAR) + part, rows(mine, token_both, part * half, half), far, dev_core)
         send(back_key(tick, PART_NEAR), rows(mine, token_core), core_in.at[tick, 0], dev_core)
 
     def pair_sum(tick):
-        arrived(back_key(tick, PART_FAR), core_in.at[tick, 1])
-        own = rows(back_partial.at[tick], token_cross)[...].astype(F32)
-        pair_out[tick] = (own + core_in[tick, 1].astype(F32)).astype(BF16)
-        send(back_key(tick, PAIR), pair_out.at[tick], pair_in.at[tick], dev_cross)
+        for part in range(2):
+            at = pl.ds(part * half, half)
+            arrived(back_key(tick, PART_FAR) + part, core_in.at[tick, 1, at])
+            own = rows(back_partial.at[tick], token_cross, part * half, half)[...].astype(F32)
+            pair_out[tick, at] = (own + core_in[tick, 1, at].astype(F32)).astype(BF16)
+            send(back_key(tick, PAIR) + part, pair_out.at[tick, at], pair_in.at[tick, at], dev_cross)
 
     def home_sum(tick):
         arrived(back_key(tick, PART_NEAR), core_in.at[tick, 0])
-        arrived(back_key(tick, PAIR), pair_in.at[tick])
-        own = rows(back_partial.at[tick], token)[...].astype(F32)
-        home_out[tick] = (own + core_in[tick, 0].astype(F32) + pair_in[tick].astype(F32)).astype(BF16)
-        key = back_key(tick, HOME)
-
-        @pl.when(diagonal)
-        def _():
-            pltpu.make_async_copy(home_out.at[tick], home_in.at[tick], recv_sem.at[key]).start()
-
-        @pl.when(jnp.logical_not(diagonal))
-        def _():
-            send(key, home_out.at[tick], home_in.at[tick], dev_home)
-
-    def gradient(tick, coming):
-        arrived(back_key(tick, HOME), home_in.at[tick])
-        return (coming.astype(F32) + home_in[tick].astype(F32)).astype(BF16)
+        for part in range(2):
+            at = pl.ds(part * half, half)
+            key = back_key(tick, HOME) + part
+            arrived(back_key(tick, PAIR) + part, pair_in.at[tick, at])
+            own = rows(back_partial.at[tick], token, part * half, half)[...].astype(F32)
+            home_out[tick, at] = (own + core_in[tick, 0, at].astype(F32) + pair_in[tick, at].astype(F32)).astype(BF16)
+            if tick == 0:
+                send(key, home_out.at[tick, at], home_in.at[tick, at], (seg_prev, token, row))
+                continue
+
+            @pl.when(diagonal)
+            def _():
+                pltpu.make_async_copy(home_out.at[tick, at], home_in.at[tick, at], recv_sem.at[key]).start()
+
+            @pl.when(jnp.logical_not(diagonal))
+            def _():
+                send(key, home_out.at[tick, at], home_in.at[tick, at], dev_home)
+
+    def home_arrived(tick):
+        for part in range(2):
+            arrived(back_key(tick, HOME) + part, home_in.at[tick, pl.ds(part * half, half)])
+
+    def added(coming, term):
+        return (coming.astype(F32) + term.astype(F32)).astype(BF16)
 
     def store(at, src, dst):
         copy = pltpu.make_async_copy(src, dst, local_sem.at[at])
         copy.start()
         return copy
 
+    def wait_loads():
+        for load in loads:
+            load.wait()
+
+    stores = []
+
+    def pass_on_output():
+        result[0] = advance(FWD1, incoming[...])
+        message[...] = jnp.where(seg == segments - 1, fresh[...], result[0])
+        send(key_of(FWD2, GATHER), message.at[pl.ds(0, half)], rows(full_in.at[FWD2], row, 0, half), (seg_next, col, spot))
+        send(key_of(FWD2, GATHER) + 1, message.at[pl.ds(half, half)], rows(full_in.at[FWD2], row, half, half), (seg_next, col, spot))
+        send(SEG_OUT, message, feed, (seg_next, row, col))
+        stores.append(store(5, result.at[0], outputs_hbm.at[0]))
+
+    def pass_on_returning():
+        pl.semaphore_wait(here_sem, 2)
+        send(SEG_RETURNING, returning_hbm, returning_next, (seg_prev, row, col))
+
+    def scale_second():
+        arrived(SEG_RETURNING, returning_next)
+        home_arrived(0)
+        following = added(returning_next[...], home_in[0])
+        upstream[...] = jnp.where(seg == segments - 1, cotangent[...], following)
+        scale(1, BACK2, upstream[...])
+        send(SEG_TERM, home_in.at[0], term, (seg_next, row, col))
+
+    def finish_first():
+        arrived(SEG_TERM, term)
+        grad[0] = added(returning[...], term[...])
+        stores.append(store(6, grad.at[0], grads_hbm.at[0]))
+
+    def finish_output():
+        arrived(SEG_OUT, feed)
+        result[1] = advance(FWD2, feed[...])
+        stores.append(store(7, result.at[1], outputs_hbm.at[1]))
+
+    def finish_gradient():
+        home_arrived(1)
+        grad[1] = added(upstream[...], home_in[1])
+        stores.append(store(8, grad.at[1], grads_hbm.at[1]))
+
     gather(BACK1, stash_hbm.at[0])
     gather(FWD1, incoming_hbm)
+    share(BACK1)
     gather(BACK2, stash_hbm.at[1])
-    share(BACK1)
     share(FWD1)
     relay(BACK1)
-    for load in loads:
-        load.wait()
+    wait_loads()
+    multiply(BACK1)
     relay(FWD1)
-    multiply(BACK1)
+    share(BACK2)
     multiply(FWD1)
-    share(BACK2)
+    relay(BACK2)
     pass_sum(BACK1)
-    relay(BACK2)
     pass_sum(FWD1)
     scale(0, BACK1, returning[...])
-    result[0] = advance(FWD1, incoming[...])
-    message[...] = jnp.where(seg == segments - 1, fresh[...], result[0])
-    send(SEG_OUT, message, feed, (seg_next, row, col))
-    send(key_of(FWD2, GATHER), message, rows(full_in.at[FWD2], row), (seg_next, col, spot))
     multiply(BACK2)
+    pass_on_returning()
+    pass_on_output()
     pass_scaled(0)
-    stores = [store(5, result.at[0], outputs_hbm.at[0])]
-    share(FWD2)
     pass_sum(BACK2)
     multiply_back(0)
     pair_sum(0)
+    home_sum(0)
+    share(FWD2)
+    scale_second()
     relay(FWD2)
-    home_sum(0)
     multiply(FWD2)
-    grad[0] = gradient(0, returning[...])
-    grad_message[...] = jnp.where(seg == 0, cotangent[...], grad[0])
-    send(SEG_GRAD, grad_message, upstream, (seg_prev, row, col))
-    stores.append(store(6, grad.at[0], grads_hbm.at[0]))
-    arrived(SEG_GRAD, upstream)
-    scale(1, BACK2, upstream[...])
+    pass_scaled(1)
     pass_sum(FWD2)
-    pass_scaled(1)
-    arrived(SEG_OUT, feed)
-    result[1] = advance(FWD2, feed[...])
-    stores.append(store(7, result.at[1], outputs_hbm.at[1]))
     multiply_back(1)
+    finish_first()
     pair_sum(1)
     home_sum(1)
-    grad[1] = gradient(1, upstream[...])
-    stores.append(store(8, grad.at[1], grads_hbm.at[1]))
-
-    for stream in range(4):
-        whole = rows(full_in.at[stream], row)
-        if stream != FWD2:
-
-            @pl.when(jnp.logical_not(diagonal))
-            def _():
-                left(key_of(stream, GATHER), whole)
-        else:
-            left(key_of(stream, GATHER), whole)
-        for step in (CORE, CROSS, RELAY):
-            left(key_of(stream, step), whole)
-        for step in (HOP_UP, HOP_DOWN, LATE_UP, LATE_DOWN, SUM_UP, SUM_DOWN):
-            left(key_of(stream, step), hop_in.at[stream, 0])
-    for tick in range(2):
-        for step in (OWN_UP, OWN_DOWN, REST_UP, REST_DOWN, NEXT_UP, NEXT_DOWN):
-            left(back_key(tick, step), hop_in.at[0, 0])
-        for step in (PART_FAR, PART_NEAR, PAIR):
-            left(back_key(tick, step), pair_in.at[tick])
-
-        @pl.when(jnp.logical_not(diagonal))
-        def _():
-            left(back_key(tick, HOME), home_in.at[tick])
-
-    left(SEG_OUT, feed)
-    left(SEG_GRAD, upstream)
+    finish_output()
+    finish_gradient()
+
+    around = [key_of(stream, GATHER) + part for stream in (BACK1, FWD1, BACK2) for part in range(2)]
+    around += [back_key(1, HOME) + part for part in range(2)]
+    for key, is_half in sent.items():
+        if key not in around:
+            left(key, hop_in.at[0, 0] if is_half else home_in.at[0])
+
+    @pl.when(jnp.logical_not(diagonal))
+    def _():
+        for key in around:
+            left(key, hop_in.at[0, 0])
+
     for copy in stores:
         copy.wait()
 
@@ -411,9 +449,11 @@
             vmem(*piece),
             vmem(2, block, width),
             vmem(*piece),
+            vmem(*piece),
             pltpu.SemaphoreType.DMA((COPIES,)),
             pltpu.SemaphoreType.DMA((COPIES,)),
             pltpu.SemaphoreType.DMA((9,)),
+            pltpu.SemaphoreType.REGULAR,
         ],
         compiler_params=pltpu.CompilerParams(collective_id=0, has_side_effects=True),
     )(gains, weights, incoming, fresh, returning, cotangent, stashed)

time: 132 us -> 119 us (0.902)
  the two profiles are of different devices: /device:TPU:1 before, /device:TPU:7 now
where the time goes in v2:
time: 119 us
  Pallas kernels  115 us (97%)
  local copies, waits for them, and re-layouts  3.34 us (3%)
    pallas_call x1, Pallas kernels, relay_call(): pl.pallas_call(functools.partial(kernel, segments), out_shape=[jax.ShapeD...  115 us
    unnamed x2, local copies, waits for them, and re-layouts  3.34 us

profile of v2, /device:TPU:7, one launch (start us, length us, event | category | flops | bytes accessed | tf_op | source)
XLA Modules:
  0.0 118.7 jit_solution(8630694491720667925)
XLA Ops:
  0.6 114.7 %shard_map.86 = (bf16[2,64,1024]{2,1,0:T(8,128)(2,1)}, bf16[2,64,1024]{2,1,0:T(8,128)(2,1)}) custom-call(f32[1,1024]{1,0:T(1,128)} %gain_ref.1, bf16[1024,1024]{1,0:T(8,128)(2,1)} %bitcast.6, bf16[64,1024]{1,0:T(8,128)(2,1)} %bitcast.10, bf16[64,1024]{1,0:T(8,128)(2,1)} %fresh_hbm.1, bf16[64,1024]{1,0:T(8,128)(2,1)} %bitcast.11, ...), custom_call_target="tpu_custom_call" | custom-call | tf_op jit(solution)/shard_map/pallas_call | solution.py:423
  115.4 1.7 %copy.11 = bf16[1,2,64,1024]{3,2,1,0:T(8,128)(2,1)} copy(bf16[1,2,64,1024]{3,2,1,0:T(8,128)(2,1)} %bitcast.8) | data formatting | bytes 524288
  117.0 1.7 %copy.12 = bf16[1,2,64,1024]{3,2,1,0:T(8,128)(2,1)} copy(bf16[1,2,64,1024]{3,2,1,0:T(8,128)(2,1)} %bitcast.7) | data formatting | bytes 524288

commit v3 on v2

--- a/solution.py
+++ b/solution.py
@@ -43,8 +43,7 @@
     returning_hbm,
     cotangent_hbm,
     stash_hbm,
-    outputs_hbm,
-    grads_hbm,
+    both_hbm,
     weight,
     incoming,
     fresh,
@@ -334,7 +333,7 @@
         send(key_of(FWD2, GATHER), message.at[pl.ds(0, half)], rows(full_in.at[FWD2], row, 0, half), (seg_next, col, spot))
         send(key_of(FWD2, GATHER) + 1, message.at[pl.ds(half, half)], rows(full_in.at[FWD2], row, half, half), (seg_next, col, spot))
         send(SEG_OUT, message, feed, (seg_next, row, col))
-        stores.append(store(5, result.at[0], outputs_hbm.at[0]))
+        stores.append(store(5, result.at[0], both_hbm.at[0, 0]))
 
     def pass_on_returning():
         pl.semaphore_wait(here_sem, 2)
@@ -351,17 +350,17 @@
     def finish_first():
         arrived(SEG_TERM, term)
         grad[0] = added(returning[...], term[...])
-        stores.append(store(6, grad.at[0], grads_hbm.at[0]))
+        stores.append(store(6, grad.at[0], both_hbm.at[1, 0]))
 
     def finish_output():
         arrived(SEG_OUT, feed)
         result[1] = advance(FWD2, feed[...])
-        stores.append(store(7, result.at[1], outputs_hbm.at[1]))
+        stores.append(store(7, result.at[1], both_hbm.at[0, 1]))
 
     def finish_gradient():
         home_arrived(1)
         grad[1] = added(upstream[...], home_in[1])
-        stores.append(store(8, grad.at[1], grads_hbm.at[1]))
+        stores.append(store(8, grad.at[1], both_hbm.at[1, 1]))
 
     gather(BACK1, stash_hbm.at[0])
     gather(FWD1, incoming_hbm)
@@ -374,27 +373,27 @@
     relay(FWD1)
     share(BACK2)
     multiply(FWD1)
+    pass_sum(BACK1)
     relay(BACK2)
-    pass_sum(BACK1)
     pass_sum(FWD1)
     scale(0, BACK1, returning[...])
     multiply(BACK2)
     pass_on_returning()
+    pass_scaled(0)
     pass_on_output()
-    pass_scaled(0)
-    pass_sum(BACK2)
     multiply_back(0)
     pair_sum(0)
+    pass_sum(BACK2)
     home_sum(0)
     share(FWD2)
     scale_second()
     relay(FWD2)
+    pass_scaled(1)
     multiply(FWD2)
-    pass_scaled(1)
+    multiply_back(1)
     pass_sum(FWD2)
-    multiply_back(1)
+    pair_sum(1)
     finish_first()
-    pair_sum(1)
     home_sum(1)
     finish_output()
     finish_gradient()
@@ -422,9 +421,9 @@
     vmem = lambda *shape: pltpu.VMEM(shape, BF16)
     return pl.pallas_call(
         functools.partial(kernel, segments),
-        out_shape=[jax.ShapeDtypeStruct((2,) + piece, BF16)] * 2,
+        out_shape=jax.ShapeDtypeStruct((2, 2) + piece, BF16),
         in_specs=[pl.BlockSpec(memory_space=pltpu.VMEM)] + [hbm] * 6,
-        out_specs=[hbm] * 2,
+        out_specs=hbm,
         scratch_shapes=[
             vmem(width, width),
             vmem(*piece),
@@ -463,7 +462,7 @@
     segments = mesh.shape["segment"]
 
     def shards(weights, layer_gains, incoming, fresh_batch, returning, fresh_cotangent, stashed_inputs):
-        outputs, grads = relay_call(
+        both = relay_call(
             segments,
             weights[0],
             layer_gains,
@@ -473,7 +472,7 @@
             fresh_cotangent,
             stashed_inputs[0],
         )
-        return outputs[None], grads[None]
+        return both[0][None], both[1][None]
 
     in_specs = (
         P("segment", "row", "col"),

time: 119 us -> 111 us (0.933)
  the two profiles are of different devices: /device:TPU:7 before, /device:TPU:1 now
where the time goes in v3:
time: 111 us; the launch traced here: 110 us
  Pallas kernels  108 us (97%)
  local copies, waits for them, and re-layouts  1.85 us (2%)
    pallas_call x1, Pallas kernels, relay_call(): pl.pallas_call(functools.partial(kernel, segments), out_shape=jax.ShapeDt...  108 us

profile of v3, /device:TPU:1, one launch (start us, length us, event | category | flops | bytes accessed | tf_op | source)
XLA Modules:
  0.0 110.4 jit_solution(18028152654841071417)
XLA Ops:
  0.6 107.9 %shard_map.86 = bf16[2,2,64,1024]{3,2,1,0:T(8,128)(2,1)} custom-call(f32[1,1024]{1,0:T(1,128)} %gain_ref.1, bf16[1024,1024]{1,0:T(8,128)(2,1)} %bitcast.4, bf16[64,1024]{1,0:T(8,128)(2,1)} %bitcast.6, bf16[64,1024]{1,0:T(8,128)(2,1)} %fresh_hbm.1, bf16[64,1024]{1,0:T(8,128)(2,1)} %bitcast.7, bf16[64,1024]{1,0:T(8,128)(2,1)} %cotangent_hbm.1, ...), custom_call_target="tpu_custom_call" | custom-call | tf_op jit(solution)/shard_map/pallas_call | solution.py:422
  108.6 1.9 %fusion = (bf16[1,2,64,1024]{3,2,1,0:T(8,128)(2,1)}, bf16[1,2,64,1024]{3,2,1,0:T(8,128)(2,1)}) fusion(bf16[2,2,64,1024]{3,2,1,0:T(8,128)(2,1)} %shard_map.86), kind=kLoop, calls=%fused_computation | loop fusion | bytes 1048576 | tf_op jit(solution)/shard_map/slice | solution.py:475

commit v4 on v3

--- a/solution.py
+++ b/solution.py
@@ -243,14 +243,20 @@
         return (own_block.astype(F32) + gain_ref[...] * (pre * jax.nn.sigmoid(pre))).astype(BF16)
 
     def scale(tick, stream, coming):
-        pre = pre_activation(stream)
-        sigma = jax.nn.sigmoid(pre)
-        slope = sigma * (1.0 + pre * (1.0 - sigma))
-        all_rows = scaled.at[tick]
-        rows(all_rows, row)[...] = (coming.astype(F32) * gain_ref[...] * slope).astype(BF16)
+        final, all_rows = last_in.at[stream], scaled.at[tick]
+        for part, keys in enumerate(((SUM_UP, LATE_DOWN), (LATE_UP, SUM_DOWN))):
+            at = pl.ds(part * half, half)
+            for side, key in enumerate(keys):
+                arrived(key_of(stream, key), final.at[side, at])
+            own = rows(partial.at[stream], row, part * half, half)[...].astype(F32)
+            pre = own + final[0, at].astype(F32) + final[1, at].astype(F32)
+            sigma = jax.nn.sigmoid(pre)
+            slope = sigma * (1.0 + pre * (1.0 - sigma))
+            came = coming[part * half : (part + 1) * half].astype(F32)
+            piece = rows(all_rows, row, part * half, half)
+            piece[...] = (came * gain_ref[...] * slope).astype(BF16)
+            send(back_key(tick, (OWN_UP, OWN_DOWN)[part]), piece, piece, (dev_up, dev_down)[part])
         low, high = rows(all_rows, row, 0, half), rows(all_rows, row, half, half)
-        send(back_key(tick, OWN_UP), low, low, dev_up)
-        send(back_key(tick, OWN_DOWN), high, high, dev_down)
         send(back_key(tick, REST_UP), high, high, dev_up)
         send(back_key(tick, REST_DOWN), low, low, dev_down)
 
@@ -372,8 +378,8 @@
     multiply(BACK1)
     relay(FWD1)
     share(BACK2)
+    pass_sum(BACK1)
     multiply(FWD1)
-    pass_sum(BACK1)
     relay(BACK2)
     pass_sum(FWD1)
     scale(0, BACK1, returning[...])
@@ -391,10 +397,10 @@
     pass_scaled(1)
     multiply(FWD2)
     multiply_back(1)
+    pair_sum(1)
     pass_sum(FWD2)
-    pair_sum(1)
+    home_sum(1)
     finish_first()
-    home_sum(1)
     finish_output()
     finish_gradient()
 

time: 111 us -> 112 us (level)
  the two profiles are of different devices: /device:TPU:1 before, /device:TPU:114 now
where the time goes in v4:
time: 112 us
  Pallas kernels  109 us (97%)
  local copies, waits for them, and re-layouts  1.85 us (2%)
    pallas_call x1, Pallas kernels, relay_call(): pl.pallas_call(functools.partial(kernel, segments), out_shape=jax.ShapeDt...  109 us

profile of v4, /device:TPU:114, one launch (start us, length us, event | category | flops | bytes accessed | tf_op | source)
XLA Modules:
  0.0 111.9 jit_solution(1616078934073096419)
XLA Ops:
  0.6 109.4 %shard_map.86 = bf16[2,2,64,1024]{3,2,1,0:T(8,128)(2,1)} custom-call(f32[1,1024]{1,0:T(1,128)} %gain_ref.1, bf16[1024,1024]{1,0:T(8,128)(2,1)} %bitcast.4, bf16[64,1024]{1,0:T(8,128)(2,1)} %bitcast.6, bf16[64,1024]{1,0:T(8,128)(2,1)} %fresh_hbm.1, bf16[64,1024]{1,0:T(8,128)(2,1)} %bitcast.7, bf16[64,1024]{1,0:T(8,128)(2,1)} %cotangent_hbm.1, ...), custom_call_target="tpu_custom_call" | custom-call | tf_op jit(solution)/shard_map/pallas_call | solution.py:428
  110.1 1.9 %fusion = (bf16[1,2,64,1024]{3,2,1,0:T(8,128)(2,1)}, bf16[1,2,64,1024]{3,2,1,0:T(8,128)(2,1)}) fusion(bf16[2,2,64,1024]{3,2,1,0:T(8,128)(2,1)} %shard_map.86), kind=kLoop, calls=%fused_computation | loop fusion | bytes 1048576 | tf_op jit(solution)/shard_map/slice | solution.py:481
